TPU v7x, 256 devices: a whole 4x4x8 slice. The times are simulated.
256 devices in a mesh: row: 16 (over z, core), col: 16 (over x, y).
Axes of the slice: x: 4, y: 4, z: 8, core: 2. Of those that a mesh axis runs over, the one named last changes fastest.
Arguments:
- tile_values: float32 [12288, 32, 1024], P(('row', 'col')), may hold values from -6 to 6
- tile_count: int32 [256], P(('row', 'col')), may hold values from 1 to 48, as said below
- mode1_column: int32 [12288, 1], P(('row', 'col')), may hold values from 0 to 15; in each aligned block of 48 rows (0 to 47, 48 to 95, ...) at most 4 rows name the same one
- mode1_offset: int32 [12288], P(('row', 'col')), may hold values from 0 to 15
- mode2_row: int32 [12288, 1], P(('row', 'col')), may hold values from 0 to 15; in each aligned block of 48 rows (0 to 47, 48 to 95, ...) at most 4 rows name the same one
- mode2_offset: int32 [12288], P(('row', 'col')), may hold values from 0 to 7
- mode3_offset: int32 [12288], P(('row', 'col')), may hold values from 0 to 15
- mode2_factor: float32 [65536, 256], P(('row', 'col'))
- mode3_factor: float32 [8192, 256], P('col')
Outputs:
- updated: float32 [131072, 256], P(('row', 'col'))
Inputs may be any that keep to these rules, and one draw needn't show every extreme that they name: Device d's live tiles fill its first tile_count[d] slots; other slots are ignored. Some device holds 48 live tiles. `mode1_column`: at most 4 slots of one device name the same value, and some device reaches it. `mode2_row`: at most 4 slots of one device name the same value, and some device reaches it.
All inputs are finite; a program needn't handle non-finite values.
Results may differ from a plain program's by a relative error of at most 0.0003.
Values sent between devices are 32-bit elements; how exact they have to be, the bound alone decides.
No kernel may reach another device: no remote copies, remote signals or barrier semaphores. Data moves between devices by JAX's collectives and lax.ppermute only.
A program may use at most 128 MiB of HBM per device.

v0:
```python
import jax
import jax.numpy as jnp
from jax import lax
from jax.sharding import PartitionSpec as P

IB_DEV = 16
HIGHEST_PRECISION = lax.Precision.HIGHEST


def product_of(left_matrix, right_matrix):
    return lax.dot_general(
        left_matrix,
        right_matrix,
        (((0,), (0,)), ((), ())),
        precision=HIGHEST_PRECISION,
        preferred_element_type=jnp.float32,
    )


def local(
    tile_values,
    tile_count,
    mode1_column,
    mode1_offset,
    mode2_row,
    mode2_offset,
    mode3_offset,
    mode2_factor,
    mode3_factor,
):
    slot_count = tile_values.shape[0]
    tile_edge = tile_values.shape[1]
    rank_width = mode2_factor.shape[1]
    rows_held = mode2_factor.shape[0]
    col_index = lax.axis_index("col")
    live_count = tile_count[0]
    slot_index = jnp.arange(slot_count, dtype=jnp.int32)
    is_live = slot_index < live_count
    tile_lines = jnp.arange(tile_edge, dtype=jnp.int32)
    owner_row = jnp.where(is_live, mode2_row[:, 0], -1)
    owner_col = jnp.where(is_live, mode1_column[:, 0], -1)
    own_second = product_of(mode2_factor, mode2_factor)
    own_third = product_of(mode3_factor, mode3_factor)
    sum_second = lax.psum(own_second, ("row", "col"))
    sum_third = lax.psum(own_third, "col")
    normal_matrix = sum_second * sum_third
    wanted = (owner_row * rows_held + mode2_offset * tile_edge)[:, None] + tile_lines[None, :]
    shard_piece = lax.all_gather(mode2_factor, "row", axis=0, tiled=True)
    piece_length = shard_piece.shape[0]
    inside = (wanted >= 0) & (wanted < piece_length)
    taken = jnp.take(shard_piece, jnp.clip(wanted, 0, piece_length - 1).reshape(-1), axis=0)
    taken = taken.reshape(slot_count, tile_edge, rank_width)
    picked = jnp.where(inside[:, :, None], taken, 0.0)
    third_index = (mode3_offset * tile_edge)[:, None] + tile_lines[None, :]
    mode3_rows = jnp.take(mode3_factor, third_index.reshape(-1), axis=0).reshape(
        slot_count, tile_edge, rank_width
    )
    group_size = min(8, slot_count)
    group_total = (live_count + group_size - 1) // group_size

    def contract(group_at, partials):
        start_slot = jnp.minimum(group_at * group_size, slot_count - group_size).astype(jnp.int32)
        second_part = lax.dynamic_slice_in_dim(picked, start_slot, group_size, 0)
        third_part = lax.dynamic_slice_in_dim(mode3_rows, start_slot, group_size, 0)
        values_part = lax.dynamic_slice_in_dim(tile_values, start_slot, group_size, 0)
        khatri = (second_part[:, :, None, :] * third_part[:, None, :, :]).reshape(
            group_size, tile_edge * tile_edge, rank_width
        )
        product_rows = jnp.einsum("gie,ger->gir", values_part, khatri, precision=HIGHEST_PRECISION)
        return lax.dynamic_update_slice_in_dim(partials, product_rows, start_slot, 0)

    partials = lax.fori_loop(
        0, group_total, contract, jnp.zeros((slot_count, tile_edge, rank_width), jnp.float32)
    )
    sent_targets = jnp.where(is_live, owner_col * IB_DEV + mode1_offset, -1).astype(jnp.float32)
    own_blocks = (col_index * IB_DEV + jnp.arange(IB_DEV, dtype=jnp.int32)).astype(jnp.float32)
    gathered_rows = lax.all_gather(partials, "col", axis=0, tiled=True)
    gathered_targets = lax.all_gather(sent_targets, "col", axis=0, tiled=True)
    selector = (gathered_targets[:, None] == own_blocks[None, :]).astype(jnp.float32)
    mttkrp = jnp.einsum("pb,pir->bir", selector, gathered_rows, precision=HIGHEST_PRECISION)
    cholesky_factor = jnp.linalg.cholesky(normal_matrix)
    mttkrp_rows = mttkrp.reshape(IB_DEV * tile_edge, rank_width)
    return jax.scipy.linalg.cho_solve((cholesky_factor, True), mttkrp_rows.T).T


def solution(mesh):
    placed = (
        P(("row", "col"), None, None),
        P(("row", "col")),
        P(("row", "col"), None),
        P(("row", "col")),
        P(("row", "col"), None),
        P(("row", "col")),
        P(("row", "col")),
        P(("row", "col"), None),
        P("col", None),
    )
    return jax.shard_map(
        local, mesh=mesh, in_specs=placed, out_specs=P(("row", "col"), None), check_vma=False
    )
```

profile of v0, /device:TPU:1, one launch (start us, length us, event | category | flops | bytes accessed | tf_op | source)
XLA Modules:
  0.0 551.6 jit_solution(1135849408825072373)
XLA Ops:
  8.2 2.3 fusion.31
  10.6 1.7 fusion.32
  13.7 3.7 gather_fusion.1
  17.4 1.5 broadcast_select_fusion
  18.8 37.9 %all-gather.3.cloned.1.call-done = f32[4096,256]{1,0:T(8,128)} async-done(((f32[256,256]{1,0:T(8,128)}), f32[4096,256]{1,0:T(8,128)}) %all-gather.3.cloned.1.call-update) | async-done | bytes 4194320 | tf_op jit(solution)/shard_map/all_gather | solution.py:48
  56.7 5.9 %gather_fusion = f32[1536,256]{1,0:T(8,128)S(1)} fusion(f32[4096,256]{1,0:T(8,128)} %all-gather.3.cloned.1.call-done, s32[2048]{0:T(1024)S(1)} %pad_clamp_fusion.1), kind=kCustom, calls=%fused_computation | custom fusion | bytes 3151872 | tf_op jit(solution)/shard_map/jit(_take)/gather | solution.py:51
  62.6 1.5 select_select_fusion
  64.2 53.0 %while.11 = (s32[]{:T(128)}, f32[48,32,256]{2,0,1:T(8,128)S(1)}, s32[]{:T(128)}, f32[48,32,1024]{2,1,0:T(8,128)}, f32[48,32,256]{2,1,0:T(8,128)}, /*index=5*/f32...) while((s32[]{:T(128)}, f32[48,32,256]{2,0,1:T(8,128)S(1)}, ...), condition=%wide.region_7.8_spmd, body=%wide.region_6.7_spmd.sunk | while | flops 807403520 | bytes 20709556 | solution.py:72
  65.3 1.2 broadcast_multiply_fusion.3
  66.5 6.1 %fusion.52 = f32[8,32,256]{2,1,0:T(8,128)S(1)} fusion(f32[8,1024,256]{2,1,0:T(8,128)S(1)} %bitcast.78, f32[48,32,1024]{2,1,0:T(8,128)} %get-tuple-element.177, s32[]{:T(128)S(6)} %select_n.118), kind=kOutput, calls=%fused_computation.3.clone.1 | convolution fusion | flops 805306368 | bytes 9699332 | tf_op jit(solution)/shard_map/while/body/gie,ger->gir/dot_general | solution.py:69
  74.2 1.2 broadcast_multiply_fusion.3
  75.3 6.1 %fusion.52 = f32[8,32,256]{2,1,0:T(8,128)S(1)} fusion(f32[8,1024,256]{2,1,0:T(8,128)S(1)} %bitcast.78, f32[48,32,1024]{2,1,0:T(8,128)} %get-tuple-element.177, s32[]{:T(128)S(6)} %select_n.118), kind=kOutput, calls=%fused_computation.3.clone.1 | convolution fusion | flops 805306368 | bytes 9699332 | tf_op jit(solution)/shard_map/while/body/gie,ger->gir/dot_general | solution.py:69
  83.0 1.2 broadcast_multiply_fusion.3
  84.2 6.1 %fusion.52 = f32[8,32,256]{2,1,0:T(8,128)S(1)} fusion(f32[8,1024,256]{2,1,0:T(8,128)S(1)} %bitcast.78, f32[48,32,1024]{2,1,0:T(8,128)} %get-tuple-element.177, s32[]{:T(128)S(6)} %select_n.118), kind=kOutput, calls=%fused_computation.3.clone.1 | convolution fusion | flops 805306368 | bytes 9699332 | tf_op jit(solution)/shard_map/while/body/gie,ger->gir/dot_general | solution.py:69
  91.9 1.2 broadcast_multiply_fusion.3
  93.0 6.1 %fusion.52 = f32[8,32,256]{2,1,0:T(8,128)S(1)} fusion(f32[8,1024,256]{2,1,0:T(8,128)S(1)} %bitcast.78, f32[48,32,1024]{2,1,0:T(8,128)} %get-tuple-element.177, s32[]{:T(128)S(6)} %select_n.118), kind=kOutput, calls=%fused_computation.3.clone.1 | convolution fusion | flops 805306368 | bytes 9699332 | tf_op jit(solution)/shard_map/while/body/gie,ger->gir/dot_general | solution.py:69
  100.7 1.2 broadcast_multiply_fusion.3
  101.8 6.1 %fusion.52 = f32[8,32,256]{2,1,0:T(8,128)S(1)} fusion(f32[8,1024,256]{2,1,0:T(8,128)S(1)} %bitcast.78, f32[48,32,1024]{2,1,0:T(8,128)} %get-tuple-element.177, s32[]{:T(128)S(6)} %select_n.118), kind=kOutput, calls=%fused_computation.3.clone.1 | convolution fusion | flops 805306368 | bytes 9699332 | tf_op jit(solution)/shard_map/while/body/gie,ger->gir/dot_general | solution.py:69
  110.7 6.1 %fusion.52 = f32[8,32,256]{2,1,0:T(8,128)S(1)} fusion(f32[8,1024,256]{2,1,0:T(8,128)S(1)} %bitcast.78, f32[48,32,1024]{2,1,0:T(8,128)} %get-tuple-element.177, s32[]{:T(128)S(6)} %select_n.118), kind=kOutput, calls=%fused_computation.3.clone.1 | convolution fusion | flops 805306368 | bytes 9699332 | tf_op jit(solution)/shard_map/while/body/gie,ger->gir/dot_general | solution.py:69
  117.3 1.2 copy-done.1
  119.8 29.3 %all-reduce.1 = f32[768]{0:T(1024)S(1)} all-reduce(f32[768]{0:T(1024)S(1)} %convert_dynamic-update-slice_fusion), channel_id=1, replica_groups=mesh['row'=16,'col'=16] {'col'}, use_global_device_ids=true, to_apply=%add.1 | all-reduce | flops 768 | bytes 6144
  149.1 120.2 %all-reduce.5.cloned.1.call-done = f32[256,256]{0,1:T(8,128)} async-done(((f32[256,256]{0,1:T(8,128)}), f32[256,256]{0,1:T(8,128)}) %all-reduce.5.cloned.1.call-update) | async-done | bytes 262160 | tf_op jit(solution)/shard_map/psum | solution.py:44
  269.4 95.4 %all-reduce.7.cloned.1.call-done = f32[256,256]{0,1:T(8,128)} async-done(((f32[256,256]{0,1:T(8,128)}), f32[256,256]{0,1:T(8,128)}) %all-reduce.7.cloned.1.call-update) | async-done | bytes 262160 | tf_op jit(solution)/shard_map/psum | solution.py:45
  366.0 11.7 %cholesky.50 = f32[128,128]{1,0:T(8,128)S(1)} custom-call(f32[128,128]{1,0:T(8,128)S(1)} %cholesky.118), custom_call_target="Cholesky" | custom-call | tf_op jit(solution)/shard_map/jit(cholesky)/cholesky | solution.py:81
  377.8 9.8 %custom-call.18 = f32[1,128,128]{1,2,0:T(8,128)S(1)} custom-call(f32[1,128,128]{2,1,0:T(8,128)S(1)} %get-tuple-element.74), custom_call_target="InvertDiagBlocksLowerTriangular" | custom-call | tf_op jit(solution)/shard_map/jit(cholesky)/cholesky | solution.py:81
  388.1 11.7 %cholesky.105 = f32[128,128]{1,0:T(8,128)S(1)} custom-call(f32[128,128]{1,0:T(8,128)S(1)} %convolution_subtract_fusion.2), custom_call_target="Cholesky" | custom-call | tf_op jit(solution)/shard_map/jit(cholesky)/cholesky | solution.py:81
  402.0 4.3 while.12
  402.8 1.4 bitcast_dynamic-update-slice_fusion.2
  404.9 1.4 bitcast_dynamic-update-slice_fusion.2
  406.3 19.7 %custom-call.19 = f32[2,128,128]{1,2,0:T(8,128)S(1)} custom-call(f32[2,128,128]{2,1,0:T(8,128)S(1)} %get-tuple-element.46), custom_call_target="InvertDiagBlocksLowerTriangular" | custom-call | tf_op jit(solution)/shard_map/jit(_cho_solve)/triangular_solve | solution.py:83
  426.0 101.7 %all-gather.5.cloned.1.call-done = f32[768,32,256]{2,0,1:T(8,128)} async-done(((f32[48,32,256]{2,0,1:T(8,128)}), f32[768,32,256]{2,0,1:T(8,128)}) %all-gather.5.cloned.1.call-update) | async-done | bytes 25165840 | tf_op jit(solution)/shard_map/all_gather | solution.py:77
  527.7 12.3 %fusion.14 = f32[16,32,256]{2,0,1:T(8,128)S(1)} fusion(f32[768,32,256]{2,0,1:T(8,128)} %all-gather.5.cloned.1.call-done, f32[768]{0:T(1024)S(1)} %all-reduce.1, f32[16]{0:T(128)S(1)} %add_convert_fusion), kind=kOutput, calls=%fused_computation.39 | convolution fusion | flops 1207971840 | bytes 25693248 | tf_op jit(solution)/shard_map/pb,pir->bir/dot_general | solution.py:80
  (86 shorter events, 20.3 us)
Async XLA Ops:
  7.4 3.2 copy-start
  7.4 5.7 %copy-start.4 = (s32[48,1]{0,1:T(1,128)S(1)}, s32[48,1]{0,1:T(1,128)}, u32[]{:S(2)}) copy-start(s32[48,1]{0,1:T(1,128)} %param.15) | copy-start | bytes 580
  7.4 5.7 %copy-start.5 = (s32[48]{0:T(128)S(1)}, s32[48]{0:T(128)}, u32[]{:S(2)}) copy-start(s32[48]{0:T(128)} %param.16) | copy-start | bytes 580
  7.4 5.9 %copy-start.6 = (s32[48]{0:T(128)S(1)}, s32[48]{0:T(128)}, u32[]{:S(2)}) copy-start(s32[48]{0:T(128)} %param.17) | copy-start | bytes 580
  7.4 49.3 %all-gather.3.cloned.1.call-start = ((), (), s32[]{:S(2)}) async-start(), calls=%async_computation.2 | async-start | bytes 4456448 | tf_op jit(solution)/shard_map/all_gather | solution.py:48
  8.1 261.3 %all-reduce.5.cloned.1.call-start = ((), (), s32[]{:S(2)}) async-start(), calls=%async_computation | async-start | bytes 524288 | tf_op jit(solution)/shard_map/psum | solution.py:44
  10.5 354.3 %all-reduce.7.cloned.1.call-start = ((), (), s32[]{:S(2)}) async-start(), calls=%async_computation.1 | async-start | bytes 524288 | tf_op jit(solution)/shard_map/psum | solution.py:45
  12.3 515.3 %all-gather.5.cloned.1.call-start = ((), (), s32[]{:S(2)}) async-start(), calls=%async_computation.3 | async-start | bytes 26738688 | tf_op jit(solution)/shard_map/all_gather | solution.py:77
  117.2 1.2 copy-start.1
  117.2 1.3 copy-start.7
  117.3 2.4 copy-start.2
  117.3 2.4 copy-start.3
Sparse Core Ops, SparseCore 0:
  10.2 46.4 all-gather.2
Sparse Core Ops, SparseCore 1:
  14.0 255.3 all-reduce.4
  272.4 92.3 all-reduce.6
  367.4 160.2 all-gather.4
where the time goes:
time: 552 us
  waiting for transfers between devices  356 us (64%)
  other arithmetic  65.2 us (12%)
  matrix products  56.1 us (10%)
  blocking collectives  29.3 us (5%)
  local copies, waits for them, and re-layouts  26.3 us (5%)
  between operations  18 us (3%)
    psum x1, waiting for transfers between devices, local(): sum_second = lax.psum(own_second, ('row', 'col'))  120 us
    all_gather x1, waiting for transfers between devices, local(): gathered_rows = lax.all_gather(partials, 'col', axis=0, tiled=True)  102 us
    psum x1, waiting for transfers between devices, local(): sum_third = lax.psum(own_third, 'col')  95.4 us
    all_gather x1, waiting for transfers between devices, local(): shard_piece = lax.all_gather(mode2_factor, 'row', axis=0, tiled=True)  37.9 us
    dot_general x6, matrix products, contract(): jnp.einsum('gie,ger->gir', values_part, khatri, precision=HIGHEST_PRECISION)  36.6 us
    another operation x6, other arithmetic, local(): cholesky_factor = jnp.linalg.cholesky(normal_matrix)  34 us
    unnamed x1, blocking collectives  29.3 us
    another operation x3, other arithmetic, local(): return jax.scipy.linalg.cho_solve((cholesky_factor, True), mttkrp_rows.T).T  19.7 us
  transfers between devices with their start and end apart: 4, of which 4 were waited for; matrix products, arithmetic and copies ran while one was open for 24% of the time, Pallas kernels for 0%

commit v1 on v0

--- a/solution.py
+++ b/solution.py
@@ -41,7 +41,7 @@
     owner_col = jnp.where(is_live, mode1_column[:, 0], -1)
     own_second = product_of(mode2_factor, mode2_factor)
     own_third = product_of(mode3_factor, mode3_factor)
-    sum_second = lax.psum(own_second, ("row", "col"))
+    sum_second = lax.psum(lax.psum(own_second, "col"), "row")
     sum_third = lax.psum(own_third, "col")
     normal_matrix = sum_second * sum_third
     wanted = (owner_row * rows_held + mode2_offset * tile_edge)[:, None] + tile_lines[None, :]

time: 552 us -> 356 us (0.64)
  waiting for transfers between devices: 356 us -> 160 us
    psum x2, waiting for transfers between devices: 216 us -> 109 us  [local(): sum_second = lax.psum(lax.psum(own_second, 'col'), 'row')]
    all_gather x1, waiting for transfers between devices: 102 us -> 50.4 us  [local(): gathered_rows = lax.all_gather(partials, 'col', axis=0, tiled=True)]
    all_gather x1, waiting for transfers between devices: 37.9 us -> 0.03 us  [local(): shard_piece = lax.all_gather(mode2_factor, 'row', axis=0, tiled=True)]
  transfers between devices with their start and end apart: 4 -> 4, of which waited for: 4 -> 3; matrix products, arithmetic and copies ran while one was open for 24% -> 35% of each run, Pallas kernels for 0% -> 0%
where the time goes in v1:
time: 356 us; the launch traced here: 355 us
  waiting for transfers between devices  160 us (45%)
  other arithmetic  65.1 us (18%)
  matrix products  56.1 us (16%)
  blocking collectives  29.2 us (8%)
  local copies, waits for them, and re-layouts  26.2 us (7%)
  between operations  17.9 us (5%)
    psum x2, waiting for transfers between devices, local(): sum_second = lax.psum(lax.psum(own_second, 'col'), 'row')  109 us
    all_gather x1, waiting for transfers between devices, local(): gathered_rows = lax.all_gather(partials, 'col', axis=0, tiled=True)  50.4 us
    dot_general x6, matrix products, contract(): jnp.einsum('gie,ger->gir', values_part, khatri, precision=HIGHEST_PRECISION)  36.6 us
    another operation x6, other arithmetic, local(): cholesky_factor = jnp.linalg.cholesky(normal_matrix)  34 us
    unnamed x1, blocking collectives  29.2 us
    another operation x3, other arithmetic, local(): return jax.scipy.linalg.cho_solve((cholesky_factor, True), mttkrp_rows.T).T  19.7 us
    dot_general x1, matrix products, local(): jnp.einsum('pb,pir->bir', selector, gathered_rows, precision=HIGHEST_PREC...  12.3 us
  transfers between devices with their start and end apart: 4, of which 3 were waited for; matrix products, arithmetic and copies ran while one was open for 35% of the time, Pallas kernels for 0%

profile of v1, /device:TPU:1, one launch (start us, length us, event | category | flops | bytes accessed | tf_op | source)
XLA Modules:
  0.0 355.2 jit_solution(15685910765210278214)
XLA Ops:
  7.4 2.4 fusion.31
  9.8 1.7 fusion.32
  13.2 3.7 %gather_fusion.1 = f32[1536,256]{1,0:T(8,128)S(1)} fusion(f32[512,256]{1,0:T(8,128)S(1)} %copy-done, s32[2048]{0:T(1024)S(1)} %pad_clamp_fusion), kind=kCustom, calls=%fused_computation.1 | custom fusion | bytes 3151872 | tf_op jit(solution)/shard_map/jit(_take)/gather | solution.py:55
  17.1 1.5 broadcast_select_fusion
  18.6 90.9 %all-reduce.8.cloned.1.call-done = (f32[256,256]{0,1:T(8,128)}, f32[256,256]{0,1:T(8,128)}) async-done(((f32[256,256]{0,1:T(8,128)}, f32[256,256]{0,1:T(8,128)}), (f32[256,256]{0,1:T(8,128)}, f32[256,256]{0,1:T(8,128)})) %all-reduce.8.cloned.1.call-update) | async-done | bytes 524304 | tf_op jit(solution)/shard_map/psum | solution.py:44
  109.6 5.8 %gather_fusion = f32[1536,256]{1,0:T(8,128)S(1)} fusion(f32[4096,256]{1,0:T(8,128)} %all-gather.3.cloned.1.call-done, s32[2048]{0:T(1024)S(1)} %pad_clamp_fusion.1), kind=kCustom, calls=%fused_computation | custom fusion | bytes 3151872 | tf_op jit(solution)/shard_map/jit(_take)/gather | solution.py:51
  115.5 1.5 select_select_fusion
  117.1 53.0 %while.11 = (s32[]{:T(128)}, f32[48,32,256]{2,0,1:T(8,128)S(1)}, s32[]{:T(128)}, f32[48,32,1024]{2,1,0:T(8,128)}, f32[48,32,256]{2,1,0:T(8,128)}, /*index=5*/f32...) while((s32[]{:T(128)}, f32[48,32,256]{2,0,1:T(8,128)S(1)}, ...), condition=%wide.region_8.9_spmd, body=%wide.region_7.8_spmd.sunk | while | flops 807403520 | bytes 20709564 | solution.py:72
  118.2 1.2 broadcast_multiply_fusion.3
  119.4 6.1 %fusion.52 = f32[8,32,256]{2,1,0:T(8,128)S(1)} fusion(f32[8,1024,256]{2,1,0:T(8,128)S(1)} %bitcast.78, f32[48,32,1024]{2,1,0:T(8,128)} %get-tuple-element.179, s32[]{:T(128)S(6)} %select_n.118), kind=kOutput, calls=%fused_computation.3.clone.1 | convolution fusion | flops 805306368 | bytes 9699332 | tf_op jit(solution)/shard_map/while/body/gie,ger->gir/dot_general | solution.py:69
  127.1 1.2 broadcast_multiply_fusion.3
  128.2 6.1 %fusion.52 = f32[8,32,256]{2,1,0:T(8,128)S(1)} fusion(f32[8,1024,256]{2,1,0:T(8,128)S(1)} %bitcast.78, f32[48,32,1024]{2,1,0:T(8,128)} %get-tuple-element.179, s32[]{:T(128)S(6)} %select_n.118), kind=kOutput, calls=%fused_computation.3.clone.1 | convolution fusion | flops 805306368 | bytes 9699332 | tf_op jit(solution)/shard_map/while/body/gie,ger->gir/dot_general | solution.py:69
  135.9 1.2 broadcast_multiply_fusion.3
  137.1 6.1 %fusion.52 = f32[8,32,256]{2,1,0:T(8,128)S(1)} fusion(f32[8,1024,256]{2,1,0:T(8,128)S(1)} %bitcast.78, f32[48,32,1024]{2,1,0:T(8,128)} %get-tuple-element.179, s32[]{:T(128)S(6)} %select_n.118), kind=kOutput, calls=%fused_computation.3.clone.1 | convolution fusion | flops 805306368 | bytes 9699332 | tf_op jit(solution)/shard_map/while/body/gie,ger->gir/dot_general | solution.py:69
  144.7 1.2 broadcast_multiply_fusion.3
  145.9 6.1 %fusion.52 = f32[8,32,256]{2,1,0:T(8,128)S(1)} fusion(f32[8,1024,256]{2,1,0:T(8,128)S(1)} %bitcast.78, f32[48,32,1024]{2,1,0:T(8,128)} %get-tuple-element.179, s32[]{:T(128)S(6)} %select_n.118), kind=kOutput, calls=%fused_computation.3.clone.1 | convolution fusion | flops 805306368 | bytes 9699332 | tf_op jit(solution)/shard_map/while/body/gie,ger->gir/dot_general | solution.py:69
  153.6 1.2 broadcast_multiply_fusion.3
  154.7 6.1 %fusion.52 = f32[8,32,256]{2,1,0:T(8,128)S(1)} fusion(f32[8,1024,256]{2,1,0:T(8,128)S(1)} %bitcast.78, f32[48,32,1024]{2,1,0:T(8,128)} %get-tuple-element.179, s32[]{:T(128)S(6)} %select_n.118), kind=kOutput, calls=%fused_computation.3.clone.1 | convolution fusion | flops 805306368 | bytes 9699332 | tf_op jit(solution)/shard_map/while/body/gie,ger->gir/dot_general | solution.py:69
  162.4 1.2 broadcast_multiply_fusion.3
  163.5 6.1 %fusion.52 = f32[8,32,256]{2,1,0:T(8,128)S(1)} fusion(f32[8,1024,256]{2,1,0:T(8,128)S(1)} %bitcast.78, f32[48,32,1024]{2,1,0:T(8,128)} %get-tuple-element.179, s32[]{:T(128)S(6)} %select_n.118), kind=kOutput, calls=%fused_computation.3.clone.1 | convolution fusion | flops 805306368 | bytes 9699332 | tf_op jit(solution)/shard_map/while/body/gie,ger->gir/dot_general | solution.py:69
  170.1 1.2 copy-done.1
  172.8 29.2 %all-reduce.1 = f32[768]{0:T(1024)S(1)} all-reduce(f32[768]{0:T(1024)S(1)} %convert_dynamic-update-slice_fusion), channel_id=1, replica_groups=mesh['row'=16,'col'=16] {'col'}, use_global_device_ids=true, to_apply=%add.1 | all-reduce | flops 768 | bytes 6144
  201.9 18.2 %all-reduce.6.cloned.1.call-done = f32[256,256]{0,1:T(8,128)} async-done(((f32[256,256]{0,1:T(8,128)}), f32[256,256]{0,1:T(8,128)}) %all-reduce.6.cloned.1.call-update) | async-done | bytes 262160 | tf_op jit(solution)/shard_map/psum | solution.py:44
  221.3 11.7 %cholesky.50 = f32[128,128]{1,0:T(8,128)S(1)} custom-call(f32[128,128]{1,0:T(8,128)S(1)} %cholesky.118), custom_call_target="Cholesky" | custom-call | tf_op jit(solution)/shard_map/jit(cholesky)/cholesky | solution.py:81
  233.1 9.8 %custom-call.18 = f32[1,128,128]{1,2,0:T(8,128)S(1)} custom-call(f32[1,128,128]{2,1,0:T(8,128)S(1)} %get-tuple-element.76), custom_call_target="InvertDiagBlocksLowerTriangular" | custom-call | tf_op jit(solution)/shard_map/jit(cholesky)/cholesky | solution.py:81
  243.4 11.7 %cholesky.105 = f32[128,128]{1,0:T(8,128)S(1)} custom-call(f32[128,128]{1,0:T(8,128)S(1)} %convolution_subtract_fusion.2), custom_call_target="Cholesky" | custom-call | tf_op jit(solution)/shard_map/jit(cholesky)/cholesky | solution.py:81
  257.2 4.1 %while.12 = (s32[]{:T(128)}, f32[256,256]{1,0:T(8,128)S(1)}, s32[2,2]{1,0:T(2,128)S(1)}, f32[2,128,128]{2,1,0:T(8,128)S(1)}, s32[]{:T(128)}) while((s32[]{:T(128)}, f32[256,256]{1,0:T(8,128)S(1)}, s32[2,2]{1,0:T(2,128)S(1)}, f32[2,128,128]{2,1,0:T(8,128)S(1)}, s32[]{:T(128)}) %tuple.43), condition=%wide.while_cond, body=%wide.while_body.sunk | while | flops 2 | bytes 131189 | solution.py:83
  258.0 1.4 bitcast_dynamic-update-slice_fusion.2
  260.0 1.4 bitcast_dynamic-update-slice_fusion.2
  261.3 19.7 %custom-call.19 = f32[2,128,128]{1,2,0:T(8,128)S(1)} custom-call(f32[2,128,128]{2,1,0:T(8,128)S(1)} %get-tuple-element.46), custom_call_target="InvertDiagBlocksLowerTriangular" | custom-call | tf_op jit(solution)/shard_map/jit(_cho_solve)/triangular_solve | solution.py:83
  281.0 50.4 %all-gather.5.cloned.1.call-done = f32[768,32,256]{2,0,1:T(8,128)} async-done(((f32[48,32,256]{2,0,1:T(8,128)}), f32[768,32,256]{2,0,1:T(8,128)}) %all-gather.5.cloned.1.call-update) | async-done | bytes 25165840 | tf_op jit(solution)/shard_map/all_gather | solution.py:77
  331.4 12.3 %fusion.14 = f32[16,32,256]{2,0,1:T(8,128)S(1)} fusion(f32[768,32,256]{2,0,1:T(8,128)} %all-gather.5.cloned.1.call-done, f32[768]{0:T(1024)S(1)} %all-reduce.1, f32[16]{0:T(128)S(1)} %add_convert_fusion), kind=kOutput, calls=%fused_computation.39 | convolution fusion | flops 1207971840 | bytes 25693248 | tf_op jit(solution)/shard_map/pb,pir->bir/dot_general | solution.py:80
  (88 shorter events, 18.9 us)
Async XLA Ops:
  7.4 2.4 copy-start
  7.4 5.4 %copy-start.5 = (s32[48,1]{0,1:T(1,128)S(1)}, s32[48,1]{0,1:T(1,128)}, u32[]{:S(2)}) copy-start(s32[48,1]{0,1:T(1,128)} %param.15) | copy-start | bytes 580
  7.4 5.5 %copy-start.6 = (s32[48]{0:T(128)S(1)}, s32[48]{0:T(128)}, u32[]{:S(2)}) copy-start(s32[48]{0:T(128)} %param.16) | copy-start | bytes 580
  7.4 5.6 %copy-start.7 = (s32[48]{0:T(128)S(1)}, s32[48]{0:T(128)}, u32[]{:S(2)}) copy-start(s32[48]{0:T(128)} %param.17) | copy-start | bytes 580
  7.4 102.1 %all-reduce.8.cloned.1.call-start = ((), (), s32[]{:S(2)}) async-start(), calls=%async_computation.3 | async-start | bytes 1048576 | tf_op jit(solution)/shard_map/psum | solution.py:44
  11.5 98.1 %all-gather.3.cloned.1.call-start = ((), (), s32[]{:S(2)}) async-start(), calls=%async_computation.1 | async-start | bytes 4456448 | tf_op jit(solution)/shard_map/all_gather | solution.py:48
  12.1 208.0 %all-reduce.6.cloned.1.call-start = ((), (), s32[]{:S(2)}) async-start(), calls=%async_computation | async-start | bytes 524288 | tf_op jit(solution)/shard_map/psum | solution.py:44
  109.6 221.9 %all-gather.5.cloned.1.call-start = ((), (), s32[]{:S(2)}) async-start(), calls=%async_computation.2 | async-start | bytes 26738688 | tf_op jit(solution)/shard_map/all_gather | solution.py:77
  170.1 1.2 copy-start.1
  170.1 1.3 copy-start.8
  170.1 2.5 copy-start.3
  170.1 2.5 copy-start.4
  170.1 50.0 %copy-start.2 = (f32[256,256]{0,1:T(8,128)S(1)}, f32[256,256]{0,1:T(8,128)}, u32[]{:S(2)}) copy-start(f32[256,256]{0,1:T(8,128)} %get-tuple-element.68) | copy-start | bytes 786436
Sparse Core Ops, SparseCore 0:
  11.6 97.8 all-reduce.7
  171.5 159.9 all-gather.4
Sparse Core Ops, SparseCore 1:
  14.0 46.5 all-gather.2
  109.6 110.4 all-reduce.5
